TPU v7x, 32 devices: a whole 2x2x4 slice. The times are simulated.
32 devices in a mesh: groups: 2 (over x), seq: 16 (over z, y, core).
Axes of the slice: x: 2, y: 2, z: 4, core: 2. Of those that a mesh axis runs over, the one named last changes fastest.
Arguments:
- queries: bfloat16 [256, 2560], P(('groups', 'seq')), parts along dimension 0, may hold values from -160 to 160
- new_keys: bfloat16 [256, 2560], P(('groups', 'seq')), parts along dimension 0, may hold values from -7 to 7
- new_values: bfloat16 [256, 2560], P(('groups', 'seq')), parts along dimension 0, may hold values from -6 to 6
- cache_keys: bfloat16 [16384, 2560], P(('groups', 'seq')), parts along dimension 0, may hold values from -6 to 6
- cache_values: bfloat16 [16384, 2560], P(('groups', 'seq')), parts along dimension 0, may hold values from -6 to 6
- victims: int32 [32], P('groups'), parts along dimension 0, may hold values from 0 to 63, as said below
Outputs:
- attended: bfloat16 [256, 2560], P(('groups', 'seq')), parts along dimension 0
There are 2 independent parts, one for each index of `groups`. A program takes and returns all parts, laid end to end along the dimension named above; each array names one. Nothing has to cross between parts.
Inputs may be any that keep to these rules, and one draw needn't show every extreme that they name: `victims`: 16 distinct block ids of the cache; the first and the last block are always among them.
All inputs are finite; a program needn't handle non-finite values.
Results may differ from a plain program's by a relative error of at most 0.01.
Values may be sent and summed in bfloat16 or wider, within the bound.
A program may use at most 128 MiB of HBM per device.

v0:
```python
import math

import jax
import jax.numpy as jnp
from jax import lax
from jax.sharding import PartitionSpec as P

HD = 128
BLK = 128


def similarity(query_cols, other):
    return lax.dot_general(
        query_cols, other, (((1,), (1,)), ((), ())), preferred_element_type=jnp.float32
    )


def per_device(queries, new_keys, new_values, cache_keys, cache_values, victims):
    members = lax.axis_size("seq")
    tok_dev = queries.shape[0]
    columns = queries.shape[1]
    head_count = columns // HD
    cache_rows = cache_keys.shape[0]
    block_count = cache_rows // BLK
    block_ids = lax.axis_index("seq") * block_count + jnp.arange(block_count, dtype=jnp.int32)
    evicted = jnp.any(victims[:, None] == block_ids[None, :], axis=0)
    cache_live = jnp.repeat(jnp.logical_not(evicted), BLK)[None, :]
    everyone = lax.all_gather(queries, "seq", axis=0, tiled=True)
    total = everyone.shape[0]
    scaling = 1.0 / math.sqrt(HD)

    def scores(head):
        first_col = head * HD
        query_cols = lax.dynamic_slice_in_dim(everyone, first_col, HD, 1)
        cached = (
            similarity(query_cols, lax.dynamic_slice_in_dim(cache_keys, first_col, HD, 1)) * scaling
        )
        cached = jnp.where(cache_live, cached, -1e30)
        fresh_scores = (
            similarity(query_cols, lax.dynamic_slice_in_dim(new_keys, first_col, HD, 1)) * scaling
        )
        return (cached, fresh_scores)

    def weigh(head, cached, fresh_scores, row_top):
        first_col = head * HD
        cached_exp = jnp.where(cache_live, jnp.exp(cached - row_top[:, None]), 0.0)
        fresh_exp = jnp.exp(fresh_scores - row_top[:, None])
        row_mass = jnp.sum(cached_exp, axis=1) + jnp.sum(fresh_exp, axis=1)
        head_out = jnp.dot(
            cached_exp.astype(jnp.bfloat16),
            lax.dynamic_slice_in_dim(cache_values, first_col, HD, 1),
            preferred_element_type=jnp.float32,
        )
        head_out = head_out + jnp.dot(
            fresh_exp.astype(jnp.bfloat16),
            lax.dynamic_slice_in_dim(new_values, first_col, HD, 1),
            preferred_element_type=jnp.float32,
        )
        return (head_out, row_mass)

    empty_out = jnp.zeros((total, columns), jnp.float32)
    empty_stat = jnp.zeros((total, head_count), jnp.float32)

    def head_pass(head, carry):
        outputs, maxima, masses = carry
        cached, fresh_scores = scores(head)
        row_top = jnp.maximum(jnp.max(cached, axis=1), jnp.max(fresh_scores, axis=1))
        head_out, row_mass = weigh(head, cached, fresh_scores, row_top)
        outputs = lax.dynamic_update_slice_in_dim(outputs, head_out, head * HD, 1)
        maxima = lax.dynamic_update_slice_in_dim(maxima, row_top[:, None], head, 1)
        masses = lax.dynamic_update_slice_in_dim(masses, row_mass[:, None], head, 1)
        return (outputs, maxima, masses)

    outputs, maxima, masses = lax.fori_loop(
        0, head_count, head_pass, (empty_out, empty_stat, empty_stat)
    )
    got_out, got_max, got_mass = (
        lax.all_to_all(
            outputs.reshape(members, tok_dev, columns),
            "seq",
            split_axis=0,
            concat_axis=0,
            tiled=True,
        ),
        lax.all_to_all(
            maxima.reshape(members, tok_dev, head_count),
            "seq",
            split_axis=0,
            concat_axis=0,
            tiled=True,
        ),
        lax.all_to_all(
            masses.reshape(members, tok_dev, head_count),
            "seq",
            split_axis=0,
            concat_axis=0,
            tiled=True,
        ),
    )
    peak_max = jnp.max(got_max, axis=0)
    factor = jnp.exp(got_max - peak_max[None])
    factor = factor / jnp.sum(factor * got_mass, axis=0)[None]
    merged = jnp.einsum("pthd,pth->thd", got_out.reshape(members, tok_dev, head_count, HD), factor)
    return merged.reshape(tok_dev, columns).astype(jnp.bfloat16)


def solution(mesh):
    in_specs = (
        P(("groups", "seq"), None),
        P(("groups", "seq"), None),
        P(("groups", "seq"), None),
        P(("groups", "seq"), None),
        P(("groups", "seq"), None),
        P("groups"),
    )
    out_specs = P(("groups", "seq"), None)
    return jax.shard_map(
        per_device, mesh=mesh, in_specs=in_specs, out_specs=out_specs, check_vma=False
    )
```

profile of v0, /device:TPU:0, one launch (start us, length us, event | category | flops | bytes accessed | tf_op | source)
XLA Modules:
  0.0 170.1 jit_solution(4086784012809041473)
XLA Ops:
  0.9 25.4 %all_gather.3 = bf16[128,2560]{1,0:T(8,128)(2,1)S(1)} all-gather(bf16[8,2560]{1,0:T(8,128)(2,1)} %param.8), channel_id=1, replica_groups=mesh['groups'=2,'seq'=16] {'seq'}, dimensions={0}, use_global_device_ids=true | all-gather | bytes 696320 | tf_op jit(solution)/shard_map/all_gather | solution.py:28
  27.1 102.0 %while.18 = (s32[]{:T(128)}, bf16[128,2560]{1,0:T(8,128)(2,1)}, f32[128,20]{0,1:T(8,128)S(1)}, f32[128,20]{0,1:T(8,128)S(1)}, bf16[128,2560]{1,0:T(8,128)(2,1)S(...) while((s32[]{:T(128)}, bf16[128,2560]{1,0:T(8,128)(2,1)}, ...), condition=%wide.region_6.7_spmd.clone, body=%wide.region_1.6_spmd.clone.sunk | while | flops 34690820 | bytes 1341643 | solution.py:74
  30.7 1.5 fusion.49
  35.7 1.5 fusion.49
  40.9 1.5 fusion.49
  45.9 1.5 fusion.49
  51.0 1.6 fusion.49
  56.1 1.5 fusion.49
  58.6 1.2 fusion.46
  61.3 1.5 fusion.49
  66.4 1.5 fusion.49
  71.5 1.5 fusion.49
  76.5 1.5 fusion.49
  79.0 1.2 fusion.46
  81.6 1.5 fusion.49
  84.1 1.2 fusion.46
  86.7 1.5 fusion.49
  91.8 1.5 fusion.49
  96.9 1.5 fusion.49
  99.3 1.2 fusion.46
  102.0 1.6 fusion.49
  104.5 1.2 fusion.46
  107.1 1.5 fusion.49
  112.2 1.5 fusion.49
  117.3 1.5 fusion.49
  122.4 1.5 fusion.49
  127.5 1.5 fusion.49
  129.9 3.5 %all-to-all-start.2 = ((f32[16,1,160]{2,1,0:T(1,128)}), f32[16,1,160]{2,1,0:T(1,128)S(1)}, u32[]{:S(2)}, u32[]{:S(2)}) async-start(f32[16,1,160]{2,1,0:T(1,128)} %reshape.62), calls=%async_computation.2 | async-start | bytes 32768 | tf_op jit(solution)/shard_map/all_to_all | solution.py:92
  133.6 6.2 %all-to-all-done.2 = f32[16,1,160]{2,1,0:T(1,128)S(1)} async-done(((f32[16,1,160]{2,1,0:T(1,128)}), f32[16,1,160]{2,1,0:T(1,128)S(1)}, u32[]{:S(2)}, u32[]{:S(2)}) %all-to-all-start.2) | async-done | bytes 10272 | tf_op jit(solution)/shard_map/all_to_all | solution.py:92
  139.9 9.1 %all_to_all.15 = f32[16,1,160]{2,1,0:T(1,128)S(1)} all-to-all(f32[16,1,160]{2,1,0:T(1,128)S(1)} %reshape.60), channel_id=1, replica_groups=mesh['groups'=2,'seq'=16] {'seq'}, dimensions={0} | all-to-all | bytes 20480 | tf_op jit(solution)/shard_map/all_to_all | solution.py:85
  148.9 3.6 %all-to-all-start = ((bf16[16,8,2560]{2,1,0:T(8,128)(2,1)}), bf16[16,8,2560]{2,1,0:T(8,128)(2,1)S(1)}, u32[]{:S(2)}, u32[]{:S(2)}) async-start(bf16[16,8,2560]{2,1,0:T(8,128)(2,1)} %bitcast), calls=%async_computation | async-start | bytes 1310720 | tf_op jit(solution)/shard_map/all_to_all | solution.py:78
  154.9 14.2 %all-to-all-done = bf16[16,8,2560]{2,1,0:T(8,128)(2,1)S(1)} async-done(((bf16[16,8,2560]{2,1,0:T(8,128)(2,1)}), bf16[16,8,2560]{2,1,0:T(8,128)(2,1)S(1)}, u32[]{:S(2)}, u32[]{:S(2)}) %all-to-all-start) | async-done | bytes 655392 | tf_op jit(solution)/shard_map/all_to_all | solution.py:78
  (216 shorter events, 71.0 us)
Async XLA Ops:
  129.9 10.0 %all-to-all-start.2 = ((f32[16,1,160]{2,1,0:T(1,128)}), f32[16,1,160]{2,1,0:T(1,128)S(1)}, u32[]{:S(2)}, u32[]{:S(2)}) async-start(f32[16,1,160]{2,1,0:T(1,128)} %reshape.62), calls=%async_computation.2 | async-start | bytes 32768 | tf_op jit(solution)/shard_map/all_to_all | solution.py:92
  148.9 20.1 %all-to-all-start = ((bf16[16,8,2560]{2,1,0:T(8,128)(2,1)}), bf16[16,8,2560]{2,1,0:T(8,128)(2,1)S(1)}, u32[]{:S(2)}, u32[]{:S(2)}) async-start(bf16[16,8,2560]{2,1,0:T(8,128)(2,1)} %bitcast), calls=%async_computation | async-start | bytes 1310720 | tf_op jit(solution)/shard_map/all_to_all | solution.py:78
where the time goes:
time: 172 us; the launch traced here: 170 us
  matrix products  94.4 us (55%)
  blocking collectives  34.4 us (20%)
  waiting for transfers between devices  20.4 us (12%)
  starting transfers between devices  7.09 us (4%)
  other arithmetic  6.91 us (4%)
  local copies, waits for them, and re-layouts  6.33 us (4%)
    dot_general x40, matrix products, similarity(): lax.dot_general(query_cols, other, (((1,), (1,)), ((), ())), preferred_el...  40.3 us
    dot_general x20, matrix products, weigh(): jnp.dot(fresh_exp.astype(jnp.bfloat16), lax.dynamic_slice_in_dim(new_valu...  30.6 us
    all_gather x1, blocking collectives, per_device(): everyone = lax.all_gather(queries, 'seq', axis=0, tiled=True)  25.4 us
    dot_general x20, matrix products, weigh(): jnp.dot(cached_exp.astype(jnp.bfloat16), lax.dynamic_slice_in_dim(cache_v...  23 us
    all_to_all x1, waiting for transfers between devices, per_device(): lax.all_to_all(outputs.reshape(members, tok_dev, columns), 'seq', split_a...  14.2 us
    all_to_all x1, blocking collectives, per_device(): lax.all_to_all(maxima.reshape(members, tok_dev, head_count), 'seq', split...  9.06 us
    all_to_all x1, waiting for transfers between devices, per_device(): lax.all_to_all(masses.reshape(members, tok_dev, head_count), 'seq', split...  6.24 us
    reduce_sum x40, other arithmetic, weigh(): row_mass = jnp.sum(cached_exp, axis=1) + jnp.sum(fresh_exp, axis=1)  4.38 us
  transfers between devices with their start and end apart: 2, of which 2 were waited for; matrix products, arithmetic and copies ran while one was open for 1% of the time, Pallas kernels for 0%

commit v1 on v0

v1 whole, which is shorter than its diff:
```python
import functools
import math

import jax
import jax.numpy as jnp
from jax import lax
from jax.experimental import pallas as pl
from jax.experimental.pallas import tpu as pltpu
from jax.sharding import PartitionSpec as P

HD = 128
BLK = 128
LANES = 128
HALF = 32
ROW_TILE = 128


def factors(members):
    fc = 2 if members % 2 == 0 else 1
    rest = members // fc
    fa = rest
    for cand in range(1, rest + 1):
        if rest % cand == 0 and cand * cand >= rest:
            fa = cand
            break
    return fa, rest // fa, fc


def chunks_of(heads):
    for count in (4, 5, 2, 3):
        if heads % count == 0 and heads // count <= HALF:
            return count
    return 1 if heads <= HALF else heads


def kernel(
    dims, chunks, q_ref, nk_ref, nv_ref, vic_ref, ck_ref, cv_ref, o_ref,
    qall, kbuf, vbuf, acc, send_c, recv_c, send_b, recv_b, send_a, recv_a,
    load_sem, own_sem, gs_sem, gr_sem, rs_sem, rr_sem,
):
    fa, fb, fc = dims
    members = fa * fb * fc
    tok, columns = q_ref.shape
    heads = columns // HD
    hc = heads // chunks
    width = hc * HD
    wide = width + LANES
    rows = ck_ref.shape[0]
    keys = kbuf.shape[0]
    block_count = rows // BLK
    exponent = math.log2(math.e) / math.sqrt(HD)

    me = lax.axis_index("seq")
    c = lax.rem(me, fc)
    b = lax.rem(lax.div(me, fc), fb)
    a = lax.div(me, fc * fb)

    def index(a_, b_, c_):
        return (a_ * fb + b_) * fc + c_

    def slot(a_, b_, c_):
        return (c_ * fb + b_) * fa + a_

    a_peers = [lax.rem(a + d, fa) for d in range(1, fa)]
    b_peers = [lax.rem(b + d, fb) for d in range(1, fb)]
    c_peers = [lax.rem(c + d, fc) for d in range(1, fc)]
    devices = (
        [index(p, b, c) for p in a_peers]
        + [index(a, p, c) for p in b_peers]
        + [index(a, b, p) for p in c_peers]
    )
    na, nb, nc = fa - 1, fb - 1, fc - 1

    def cols(j):
        return pl.ds(j * width, width)

    def wcols(j):
        return pl.ds(j * wide, wide)

    barrier = pltpu.get_barrier_semaphore()
    for dev in devices:
        pl.semaphore_signal(
            barrier, inc=1, device_id={"seq": dev}, device_id_type=pl.DeviceIdType.MESH
        )

    loads = []
    for j in range(chunks):
        pair = (
            pltpu.make_async_copy(
                ck_ref.at[:, cols(j)], kbuf.at[pl.ds(0, rows), cols(j)], load_sem.at[j, 0]
            ),
            pltpu.make_async_copy(
                cv_ref.at[:, cols(j)], vbuf.at[pl.ds(0, rows), cols(j)], load_sem.at[j, 1]
            ),
        )
        loads.append(pair)
    own_slot = slot(a, b, c)
    own = pltpu.make_async_copy(q_ref, qall.at[own_slot], own_sem)
    own.start()

    def remote(src, dst, sems, recvs, j, k):
        return pltpu.make_async_remote_copy(
            src_ref=src,
            dst_ref=dst,
            send_sem=sems.at[j, k],
            recv_sem=recvs.at[j, k],
            device_id={"seq": devices[k]},
            device_id_type=pl.DeviceIdType.MESH,
        )

    pl.semaphore_wait(barrier, len(devices))

    gather_a = [
        [
            remote(q_ref.at[:, cols(j)], qall.at[own_slot, :, cols(j)], gs_sem, gr_sem, j, k)
            for k in range(na)
        ]
        for j in range(chunks)
    ]
    for j in range(chunks):
        for copy in gather_a[j]:
            copy.start()
    for pair in loads:
        pair[0].start()
        pair[1].start()

    pad16 = 2 * tok - tok
    for src, dst in ((nk_ref, kbuf), (nv_ref, vbuf)):
        fresh = src[...].astype(jnp.float32)
        dst[pl.ds(rows, 2 * tok), :] = jnp.concatenate(
            [fresh, jnp.zeros((pad16, columns), jnp.float32)], axis=0
        ).astype(jnp.bfloat16)
        dst[pl.ds(rows + 2 * tok, keys - rows - 2 * tok), :] = jnp.zeros(
            (keys - rows - 2 * tok, columns), jnp.bfloat16
        )

    victims = vic_ref[...]
    pieces = []
    for k in range(block_count):
        hit = jnp.where(victims == me * block_count + k, 1.0, 0.0)
        hit = jnp.max(hit, axis=1, keepdims=True)
        pieces.append(jnp.broadcast_to(hit, (1, BLK)) * -1e30)
    tail = lax.broadcasted_iota(jnp.int32, (1, keys - rows), 1)
    pieces.append(jnp.where(tail < tok, 0.0, -1e30))
    bias = jnp.concatenate(pieces, axis=1)

    def gather_b(j):
        src = qall.at[pl.ds(slot(0, b, c), fa), :, cols(j)]
        return [remote(src, src, gs_sem, gr_sem, j, na + k) for k in range(nb)]

    def gather_c(j):
        src = qall.at[pl.ds(slot(0, 0, c), fa * fb), :, cols(j)]
        return [remote(src, src, gs_sem, gr_sem, j, na + nb + k) for k in range(nc)]

    tile_slots = max(1, min(members, ROW_TILE // tok))
    tiles = members // tile_slots

    def lane_of(r):
        return lax.broadcasted_iota(jnp.int32, (r, LANES), 1)

    def compute(j):
        def tile(t):
            first = t * tile_slots
            r = tile_slots * tok
            lane = lane_of(r)

            def head(h, stats):
                col = pl.multiple_of(j * width + h * HD, HD)
                q = qall[pl.ds(first, tile_slots), :, pl.ds(col, HD)]
                q = q.astype(jnp.float32).reshape(r, HD).astype(jnp.bfloat16)
                s = lax.dot_general(
                    q, kbuf[:, pl.ds(col, HD)], (((1,), (1,)), ((), ())),
                    preferred_element_type=jnp.float32,
                )
                s = s * exponent + bias
                top = jnp.max(s, axis=1, keepdims=True)
                top = top.astype(jnp.bfloat16).astype(jnp.float32)
                e = jnp.exp2(s - top)
                mass = jnp.sum(e, axis=1, keepdims=True)
                out = jnp.dot(
                    e.astype(jnp.bfloat16), vbuf[:, pl.ds(col, HD)],
                    preferred_element_type=jnp.float32,
                )
                at = pl.multiple_of(j * wide + h * HD, HD)
                acc[pl.ds(first, tile_slots), :, pl.ds(at, HD)] = out.reshape(tile_slots, tok, HD)
                stats = jnp.where(lane == h, top, stats)
                return jnp.where(lane == h + HALF, mass, stats)

            stats = lax.fori_loop(
                0, hc, head, jnp.zeros((r, LANES), jnp.float32), unroll=tiles == 1
            )
            acc[pl.ds(first, tile_slots), :, pl.ds(j * wide + width, LANES)] = stats.reshape(
                tile_slots, tok, LANES
            )

        if tiles == 1:
            tile(0)
        else:
            pl.loop(0, tiles)(tile)

    def encode(stats):
        high = stats.astype(jnp.bfloat16).astype(jnp.float32)
        return (high + pltpu.roll(stats - high, HALF, 1)).astype(jnp.bfloat16)

    def decode(stats):
        low = pltpu.roll(stats, LANES - HALF, 1)
        return stats + jnp.where(lane_of(stats.shape[0]) < HALF, 0.0, low)

    def pack(first, count, buf, j):
        r = count * tok
        buf[:, :, cols_w(j, width)] = acc[pl.ds(first, count), :, cols_w(j, width)].astype(
            jnp.bfloat16
        )
        stats = acc[pl.ds(first, count), :, pl.ds(j * wide + width, LANES)].reshape(r, LANES)
        buf[:, :, pl.ds(j * wide + width, LANES)] = encode(stats).reshape(count, tok, LANES)

    def cols_w(j, w):
        return pl.ds(j * wide, w)

    def merge(first, count, parts, j, last=False):
        r = count * tok
        at = pl.ds(j * wide + width, LANES)
        lane = lane_of(r)
        stats = [acc[pl.ds(first, count), :, at].reshape(r, LANES)]
        for ref in parts:
            stats.append(decode(ref[:, :, at].astype(jnp.float32).reshape(r, LANES)))
        top = functools.reduce(jnp.maximum, stats)
        factor = [jnp.exp2(s - top) for s in stats]
        mass = sum(pltpu.roll(f, HALF, 1) * s for f, s in zip(factor, stats))
        if last:
            inverse = pltpu.roll(1.0 / jnp.where(lane < HALF, 1.0, mass), LANES - HALF, 1)
            factor = [f * inverse for f in factor]
        for h in range(hc):
            here = pl.ds(j * wide + h * HD, HD)
            total = acc[pl.ds(first, count), :, here].reshape(r, HD) * factor[0][:, h : h + 1]
            for f, ref in zip(factor[1:], parts):
                total = total + ref[:, :, here].astype(jnp.float32).reshape(r, HD) * f[:, h : h + 1]
            if last:
                o_ref[:, pl.ds(j * width + h * HD, HD)] = total.astype(jnp.bfloat16)
            else:
                acc[pl.ds(first, count), :, here] = total.reshape(count, tok, HD)
        if not last:
            fused = jnp.where(lane < HALF, top, jnp.where(lane < 2 * HALF, mass, 0.0))
            acc[pl.ds(first, count), :, at] = fused.reshape(count, tok, LANES)

    def scatter_c(j):
        return [
            remote(send_c.at[k, :, :, wcols(j)], recv_c.at[k, :, :, wcols(j)], rs_sem, rr_sem, j, na + nb + k)
            for k in range(nc)
        ]

    def scatter_b(j):
        return [
            remote(send_b.at[k, :, :, wcols(j)], recv_b.at[k, :, :, wcols(j)], rs_sem, rr_sem, j, na + k)
            for k in range(nb)
        ]

    def scatter_a(j):
        return [
            remote(send_a.at[k, :, :, wcols(j)], recv_a.at[k, :, :, wcols(j)], rs_sem, rr_sem, j, k)
            for k in range(na)
        ]

    def stage_0(j):
        if j == 0:
            own.wait()
        for copy in gather_a[j]:
            copy.wait_recv()
        for copy in gather_b(j):
            copy.start()

    def stage_1(j):
        for copy in gather_b(j):
            copy.wait_recv()
        for copy in gather_c(j):
            copy.start()

    def stage_2(j):
        for copy in gather_c(j):
            copy.wait_recv()
        for copy in loads[j]:
            copy.wait()
        compute(j)
        for k, copy in enumerate(scatter_c(j)):
            pack(slot(0, 0, c_peers[k]), fa * fb, send_c.at[k], j)
            copy.start()

    def stage_3(j):
        for copy in scatter_c(j):
            copy.wait_recv()
        received = [recv_c.at[k] for k in range(nc)]
        for k, copy in enumerate(scatter_b(j)):
            first = b_peers[k] * fa
            merge(slot(0, b_peers[k], c), fa, [x.at[pl.ds(first, fa)] for x in received], j)
            pack(slot(0, b_peers[k], c), fa, send_b.at[k], j)
            copy.start()
        merge(slot(0, b, c), fa, [x.at[pl.ds(b * fa, fa)] for x in received], j)

    def stage_4(j):
        for copy in scatter_b(j):
            copy.wait_recv()
        merge(slot(0, b, c), fa, [recv_b.at[k] for k in range(nb)], j)
        for k, copy in enumerate(scatter_a(j)):
            pack(slot(a_peers[k], b, c), 1, send_a.at[k], j)
            copy.start()

    def stage_5(j):
        for copy in scatter_a(j):
            copy.wait_recv()
        merge(own_slot, 1, [recv_a.at[k] for k in range(na)], j, last=True)

    stages = (stage_0, stage_1, stage_2, stage_3, stage_4, stage_5)
    for step in range(chunks + len(stages) - 1):
        for number, stage in enumerate(stages):
            if 0 <= step - number < chunks:
                stage(step - number)
    for j in range(chunks):
        for group in (gather_a[j], gather_b(j), gather_c(j), scatter_a(j), scatter_b(j), scatter_c(j)):
            for copy in group:
                copy.wait_send()


def per_device(queries, new_keys, new_values, cache_keys, cache_values, victims):
    members = lax.axis_size("seq")
    dims = fa, fb, fc = factors(members)
    tok, columns = queries.shape
    heads = columns // HD
    chunks = chunks_of(heads)
    rows = cache_keys.shape[0]
    keys = rows + -(-2 * tok // LANES) * LANES
    total = columns + chunks * LANES
    peers = fa + fb + fc - 3
    bf16 = jnp.bfloat16
    vmem = pl.BlockSpec(memory_space=pltpu.VMEM)
    hbm = pl.BlockSpec(memory_space=pl.ANY)
    return pl.pallas_call(
        functools.partial(kernel, dims, chunks),
        out_shape=jax.ShapeDtypeStruct((tok, columns), bf16),
        in_specs=[vmem, vmem, vmem, vmem, hbm, hbm],
        out_specs=vmem,
        scratch_shapes=[
            pltpu.VMEM((members, tok, columns), bf16),
            pltpu.VMEM((keys, columns), bf16),
            pltpu.VMEM((keys, columns), bf16),
            pltpu.VMEM((members, tok, total), jnp.float32),
            pltpu.VMEM((max(1, fc - 1), fa * fb, tok, total), bf16),
            pltpu.VMEM((max(1, fc - 1), fa * fb, tok, total), bf16),
            pltpu.VMEM((max(1, fb - 1), fa, tok, total), bf16),
            pltpu.VMEM((max(1, fb - 1), fa, tok, total), bf16),
            pltpu.VMEM((max(1, fa - 1), 1, tok, total), bf16),
            pltpu.VMEM((max(1, fa - 1), 1, tok, total), bf16),
            pltpu.SemaphoreType.DMA((chunks, 2)),
            pltpu.SemaphoreType.DMA,
            pltpu.SemaphoreType.DMA((chunks, peers)),
            pltpu.SemaphoreType.DMA((chunks, peers)),
            pltpu.SemaphoreType.DMA((chunks, peers)),
            pltpu.SemaphoreType.DMA((chunks, peers)),
        ],
        compiler_params=pltpu.CompilerParams(
            collective_id=0, has_side_effects=True, vmem_limit_bytes=60 * 1024 * 1024
        ),
    )(queries, new_keys, new_values, victims.reshape(1, -1), cache_keys, cache_values)


def solution(mesh):
    row = P(("groups", "seq"), None)
    return jax.shard_map(
        per_device,
        mesh=mesh,
        in_specs=(row, row, row, row, row, P("groups")),
        out_specs=row,
        check_vma=False,
    )
```

time: 172 us -> 35.5 us (0.21)
  matrix products: 94.4 us -> 0 us
  blocking collectives: 34.4 us -> 0 us
  Pallas kernels: 0 us -> 33.8 us
  waiting for transfers between devices: 20.4 us -> 0 us
  starting transfers between devices: 7.09 us -> 0 us
  other arithmetic: 6.91 us -> 0 us
  local copies, waits for them, and re-layouts: 6.33 us -> 1.4 us
    dot_general x81 -> x0, matrix products: 94.4 us -> none  [the longest x40 40.3 us: similarity(): lax.dot_general(query_cols, other, (((1,), (1,)), ((), ())), preferred_el...]
    pallas_call x0 -> x1, Pallas kernels: none -> 33.8 us  [per_device(): pl.pallas_call(functools.partial(kernel, dims, chunks), out_shape=jax.Sha...]
    all_gather x1 -> x0, blocking collectives: 25.4 us -> none  [per_device(): everyone = lax.all_gather(queries, 'seq', axis=0, tiled=True)]
    all_to_all x2 -> x0, waiting for transfers between devices: 20.4 us -> none  [the longest x1 14.2 us: per_device(): lax.all_to_all(outputs.reshape(members, tok_dev, columns), 'seq', split_a...]
    all_to_all x1 -> x0, blocking collectives: 9.06 us -> none  [per_device(): lax.all_to_all(maxima.reshape(members, tok_dev, head_count), 'seq', split...]
    all_to_all x2 -> x0, starting transfers between devices: 7.09 us -> none  [the longest x1 3.59 us: per_device(): lax.all_to_all(outputs.reshape(members, tok_dev, columns), 'seq', split_a...]
    reduce_sum x41 -> x0, other arithmetic: 4.41 us -> none  [the longest x40 4.38 us: weigh(): row_mass = jnp.sum(cached_exp, axis=1) + jnp.sum(fresh_exp, axis=1)]
    broadcast_in_dim x21 -> x0, local copies, waits for them, and re-layouts: 2.33 us -> none  [the longest x20 1.45 us: weigh(): cached_exp = jnp.where(cache_live, jnp.exp(cached - row_top[:, None]), 0.0)]
  transfers between devices with their start and end apart: 2 -> 0, of which waited for: 2 -> 0; matrix products, arithmetic and copies ran while one was open for 1% -> 0% of each run, Pallas kernels for 0% -> 0%
where the time goes in v1:
time: 35.5 us; the launch traced here: 35.2 us
  Pallas kernels  33.8 us (95%)
  local copies, waits for them, and re-layouts  1.4 us (4%)
    pallas_call x1, Pallas kernels, per_device(): pl.pallas_call(functools.partial(kernel, dims, chunks), out_shape=jax.Sha...  33.8 us
    unnamed x1, local copies, waits for them, and re-layouts  1.4 us

profile of v1, /device:TPU:0, one launch (start us, length us, event | category | flops | bytes accessed | tf_op | source)
XLA Modules:
  0.0 35.2 jit_solution(4341614625673262294)
XLA Ops:
  0.0 33.8 %shard_map.64 = bf16[8,2560]{1,0:T(8,128)(2,1)} custom-call(bf16[8,2560]{1,0:T(8,128)(2,1)} %q_ref.1, bf16[8,2560]{1,0:T(8,128)(2,1)} %nk_ref.1, bf16[8,2560]{1,0:T(8,128)(2,1)} %nv_ref.1, s32[1,16]{1,0:T(1,128)} %bitcast.1, bf16[512,2560]{1,0:T(8,128)(2,1)} %ck_ref.1, bf16[512,2560]{1,0:T(8,128)(2,1)} %cv_ref.1), custom_call_target="tpu_custom_call" | custom-call | tf_op jit(solution)/shard_map/pallas_call | solution.py:336
  33.8 1.4 %copy.8 = bf16[8,2560]{1,0:T(8,128)(2,1)} copy(bf16[8,2560]{1,0:T(8,128)(2,1)} %shard_map.64) | data formatting | bytes 81920

commit v2 on v1

--- a/solution.py
+++ b/solution.py
@@ -13,6 +13,8 @@
 LANES = 128
 HALF = 32
 ROW_TILE = 128
+OFFSETS = (0.0, 5.0, 7.3, 9.0, 12.0, 16.0)
+STEP = 5.0
 
 
 def factors(members):
@@ -34,13 +36,13 @@
 
 
 def kernel(
-    dims, chunks, q_ref, nk_ref, nv_ref, vic_ref, ck_ref, cv_ref, o_ref,
-    qall, kbuf, vbuf, acc, send_c, recv_c, send_b, recv_b, send_a, recv_a,
-    load_sem, own_sem, gs_sem, gr_sem, rs_sem, rr_sem,
+    dims, chunks, q_hbm, nk_hbm, nv_hbm, vic_hbm, ck_ref, cv_ref, o_ref,
+    nk_ref, nv_ref, vic_ref, qall, kbuf, vbuf, acc, send_c, recv_c, send_b, recv_b, send_a, recv_a,
+    load_sem, small_sem, gs_sem, gr_sem, rs_sem, rr_sem,
 ):
     fa, fb, fc = dims
     members = fa * fb * fc
-    tok, columns = q_ref.shape
+    tok, columns = q_hbm.shape
     heads = columns // HD
     hc = heads // chunks
     width = hc * HD
@@ -61,9 +63,25 @@
     def slot(a_, b_, c_):
         return (c_ * fb + b_) * fa + a_
 
-    a_peers = [lax.rem(a + d, fa) for d in range(1, fa)]
-    b_peers = [lax.rem(b + d, fb) for d in range(1, fb)]
-    c_peers = [lax.rem(c + d, fc) for d in range(1, fc)]
+    def partners(x, size):
+        if size & (size - 1):
+            return [lax.rem(x + d, size) for d in range(1, size)], [
+                lax.rem(x + size - d, size) for d in range(1, size)
+            ]
+        found = []
+        for d in range(1, size):
+            y = x
+            bit = 1
+            while bit <= d:
+                if d & bit:
+                    y = y + bit - 2 * bit * lax.rem(lax.div(y, bit), 2)
+                bit *= 2
+            found.append(y)
+        return found, found
+
+    a_peers, a_from = partners(a, fa)
+    b_peers, b_from = partners(b, fb)
+    c_peers, c_from = partners(c, fc)
     devices = (
         [index(p, b, c) for p in a_peers]
         + [index(a, p, c) for p in b_peers]
@@ -95,34 +113,57 @@
         )
         loads.append(pair)
     own_slot = slot(a, b, c)
-    own = pltpu.make_async_copy(q_ref, qall.at[own_slot], own_sem)
+    own = pltpu.make_async_copy(q_hbm, qall.at[own_slot], small_sem.at[0])
+    small = [
+        pltpu.make_async_copy(nk_hbm, nk_ref, small_sem.at[1]),
+        pltpu.make_async_copy(nv_hbm, nv_ref, small_sem.at[2]),
+        pltpu.make_async_copy(vic_hbm, vic_ref, small_sem.at[3]),
+    ]
     own.start()
-
-    def remote(src, dst, sems, recvs, j, k):
+    for copy in small:
+        copy.start()
+    for pair in loads:
+        pair[0].start()
+        pair[1].start()
+
+    def remote(src, dst, sems, recvs, j, k, target):
         return pltpu.make_async_remote_copy(
             src_ref=src,
             dst_ref=dst,
             send_sem=sems.at[j, k],
             recv_sem=recvs.at[j, k],
-            device_id={"seq": devices[k]},
+            device_id={"seq": target},
             device_id_type=pl.DeviceIdType.MESH,
         )
 
+    def gather(src, j, k, target):
+        return remote(src, src, gs_sem, gr_sem, j, k, target)
+
+    def gather_a(j):
+        src = qall.at[own_slot, :, cols(j)]
+        return [gather(src, j, k, devices[k]) for k in range(na)]
+
+    def gather_b(j, source):
+        block = own_slot if source == 0 else slot(a_from[source - 1], b, c)
+        src = qall.at[block, :, cols(j)]
+        return [gather(src, j, na + source * nb + k, devices[na + k]) for k in range(nb)]
+
+    def gather_c(j, column):
+        at_b = b if column == 0 else b_from[column - 1]
+        src = qall.at[pl.ds(slot(0, at_b, c), fa), :, cols(j)]
+        return [
+            gather(src, j, na + fa * nb + column * nc + k, devices[na + nb + k]) for k in range(nc)
+        ]
+
+    own.wait()
     pl.semaphore_wait(barrier, len(devices))
-
-    gather_a = [
-        [
-            remote(q_ref.at[:, cols(j)], qall.at[own_slot, :, cols(j)], gs_sem, gr_sem, j, k)
-            for k in range(na)
-        ]
-        for j in range(chunks)
-    ]
     for j in range(chunks):
-        for copy in gather_a[j]:
-            copy.start()
-    for pair in loads:
-        pair[0].start()
-        pair[1].start()
+        for copy in gather_a(j):
+            copy.start()
+        for copy in gather_b(j, 0):
+            copy.start()
+    for copy in small:
+        copy.wait()
 
     pad16 = 2 * tok - tok
     for src, dst in ((nk_ref, kbuf), (nv_ref, vbuf)):
@@ -143,14 +184,6 @@
     tail = lax.broadcasted_iota(jnp.int32, (1, keys - rows), 1)
     pieces.append(jnp.where(tail < tok, 0.0, -1e30))
     bias = jnp.concatenate(pieces, axis=1)
-
-    def gather_b(j):
-        src = qall.at[pl.ds(slot(0, b, c), fa), :, cols(j)]
-        return [remote(src, src, gs_sem, gr_sem, j, na + k) for k in range(nb)]
-
-    def gather_c(j):
-        src = qall.at[pl.ds(slot(0, 0, c), fa * fb), :, cols(j)]
-        return [remote(src, src, gs_sem, gr_sem, j, na + nb + k) for k in range(nc)]
 
     tile_slots = max(1, min(members, ROW_TILE // tok))
     tiles = members // tile_slots
@@ -245,39 +278,50 @@
 
     def scatter_c(j):
         return [
-            remote(send_c.at[k, :, :, wcols(j)], recv_c.at[k, :, :, wcols(j)], rs_sem, rr_sem, j, na + nb + k)
+            remote(
+                send_c.at[k, :, :, wcols(j)], recv_c.at[k, :, :, wcols(j)], rs_sem, rr_sem, j, na + nb + k,
+                devices[na + nb + k],
+            )
             for k in range(nc)
         ]
 
     def scatter_b(j):
         return [
-            remote(send_b.at[k, :, :, wcols(j)], recv_b.at[k, :, :, wcols(j)], rs_sem, rr_sem, j, na + k)
+            remote(
+                send_b.at[k, :, :, wcols(j)], recv_b.at[k, :, :, wcols(j)], rs_sem, rr_sem, j, na + k,
+                devices[na + k],
+            )
             for k in range(nb)
         ]
 
     def scatter_a(j):
         return [
-            remote(send_a.at[k, :, :, wcols(j)], recv_a.at[k, :, :, wcols(j)], rs_sem, rr_sem, j, k)
+            remote(
+                send_a.at[k, :, :, wcols(j)], recv_a.at[k, :, :, wcols(j)], rs_sem, rr_sem, j, k,
+                devices[k],
+            )
             for k in range(na)
         ]
 
     def stage_0(j):
-        if j == 0:
-            own.wait()
-        for copy in gather_a[j]:
-            copy.wait_recv()
-        for copy in gather_b(j):
+        for source in range(1, fa):
+            gather_a(j)[source - 1].wait_recv()
+            for copy in gather_b(j, source):
+                copy.start()
+        for copy in gather_c(j, 0):
             copy.start()
 
     def stage_1(j):
-        for copy in gather_b(j):
-            copy.wait_recv()
-        for copy in gather_c(j):
-            copy.start()
+        for column in range(1, fb):
+            for source in range(fa):
+                gather_b(j, source)[column - 1].wait_recv()
+            for copy in gather_c(j, column):
+                copy.start()
 
     def stage_2(j):
-        for copy in gather_c(j):
-            copy.wait_recv()
+        for column in range(fb):
+            for copy in gather_c(j, column):
+                copy.wait_recv()
         for copy in loads[j]:
             copy.wait()
         compute(j)
@@ -310,12 +354,18 @@
         merge(own_slot, 1, [recv_a.at[k] for k in range(na)], j, last=True)
 
     stages = (stage_0, stage_1, stage_2, stage_3, stage_4, stage_5)
-    for step in range(chunks + len(stages) - 1):
-        for number, stage in enumerate(stages):
-            if 0 <= step - number < chunks:
-                stage(step - number)
+    order = sorted(
+        (OFFSETS[number] + j * STEP / chunks, number, j)
+        for number in range(len(stages))
+        for j in range(chunks)
+    )
+    for _, number, j in order:
+        stages[number](j)
     for j in range(chunks):
-        for group in (gather_a[j], gather_b(j), gather_c(j), scatter_a(j), scatter_b(j), scatter_c(j)):
+        groups = [gather_a(j), scatter_a(j), scatter_b(j), scatter_c(j)]
+        groups += [gather_b(j, source) for source in range(fa)]
+        groups += [gather_c(j, column) for column in range(fb)]
+        for group in groups:
             for copy in group:
                 copy.wait_send()
 
@@ -330,15 +380,19 @@
     keys = rows + -(-2 * tok // LANES) * LANES
     total = columns + chunks * LANES
     peers = fa + fb + fc - 3
+    copies = fa - 1 + fa * (fb - 1) + fb * (fc - 1)
     bf16 = jnp.bfloat16
     vmem = pl.BlockSpec(memory_space=pltpu.VMEM)
     hbm = pl.BlockSpec(memory_space=pl.ANY)
     return pl.pallas_call(
         functools.partial(kernel, dims, chunks),
         out_shape=jax.ShapeDtypeStruct((tok, columns), bf16),
-        in_specs=[vmem, vmem, vmem, vmem, hbm, hbm],
+        in_specs=[hbm] * 6,
         out_specs=vmem,
         scratch_shapes=[
+            pltpu.VMEM((tok, columns), bf16),
+            pltpu.VMEM((tok, columns), bf16),
+            pltpu.VMEM((1, victims.shape[0]), jnp.int32),
             pltpu.VMEM((members, tok, columns), bf16),
             pltpu.VMEM((keys, columns), bf16),
             pltpu.VMEM((keys, columns), bf16),
@@ -350,9 +404,9 @@
             pltpu.VMEM((max(1, fa - 1), 1, tok, total), bf16),
             pltpu.VMEM((max(1, fa - 1), 1, tok, total), bf16),
             pltpu.SemaphoreType.DMA((chunks, 2)),
-            pltpu.SemaphoreType.DMA,
-            pltpu.SemaphoreType.DMA((chunks, peers)),
-            pltpu.SemaphoreType.DMA((chunks, peers)),
+            pltpu.SemaphoreType.DMA((4,)),
+            pltpu.SemaphoreType.DMA((chunks, copies)),
+            pltpu.SemaphoreType.DMA((chunks, copies)),
             pltpu.SemaphoreType.DMA((chunks, peers)),
             pltpu.SemaphoreType.DMA((chunks, peers)),
         ],

time: 35.5 us -> 32.6 us (0.918)
  Pallas kernels: 33.8 us -> 31.1 us
    pallas_call x1, Pallas kernels: 33.8 us -> 31.1 us  [per_device(): pl.pallas_call(functools.partial(kernel, dims, chunks), out_shape=jax.Sha...]
where the time goes in v2:
time: 32.6 us; the launch traced here: 32.5 us
  Pallas kernels  31.1 us (95%)
  local copies, waits for them, and re-layouts  1.4 us (4%)
    pallas_call x1, Pallas kernels, per_device(): pl.pallas_call(functools.partial(kernel, dims, chunks), out_shape=jax.Sha...  31.1 us
    unnamed x1, local copies, waits for them, and re-layouts  1.4 us

profile of v2, /device:TPU:0, one launch (start us, length us, event | category | flops | bytes accessed | tf_op | source)
XLA Modules:
  0.0 32.5 jit_solution(5049946459962601855)
XLA Ops:
  0.0 31.1 %shard_map.64 = bf16[8,2560]{1,0:T(8,128)(2,1)} custom-call(bf16[8,2560]{1,0:T(8,128)(2,1)} %q_hbm.1, bf16[8,2560]{1,0:T(8,128)(2,1)} %nk_hbm.1, bf16[8,2560]{1,0:T(8,128)(2,1)} %nv_hbm.1, s32[1,16]{1,0:T(1,128)} %bitcast.1, bf16[512,2560]{1,0:T(8,128)(2,1)} %ck_ref.1, bf16[512,2560]{1,0:T(8,128)(2,1)} %cv_ref.1), custom_call_target="tpu_custom_call" | custom-call | tf_op jit(solution)/shard_map/pallas_call | solution.py:387
  31.1 1.4 %copy.8 = bf16[8,2560]{1,0:T(8,128)(2,1)} copy(bf16[8,2560]{1,0:T(8,128)(2,1)} %shard_map.64) | data formatting | bytes 81920

commit v3 on v2

--- a/solution.py
+++ b/solution.py
@@ -197,14 +197,19 @@
             r = tile_slots * tok
             lane = lane_of(r)
 
-            def head(h, stats):
-                col = pl.multiple_of(j * width + h * HD, HD)
+            def scores(h):
+                col = j * width + h * HD
+                col = col if isinstance(col, int) else pl.multiple_of(col, HD)
                 q = qall[pl.ds(first, tile_slots), :, pl.ds(col, HD)]
                 q = q.astype(jnp.float32).reshape(r, HD).astype(jnp.bfloat16)
-                s = lax.dot_general(
+                return lax.dot_general(
                     q, kbuf[:, pl.ds(col, HD)], (((1,), (1,)), ((), ())),
                     preferred_element_type=jnp.float32,
                 )
+
+            def head(h, stats, s):
+                col = j * width + h * HD
+                col = col if isinstance(col, int) else pl.multiple_of(col, HD)
                 s = s * exponent + bias
                 top = jnp.max(s, axis=1, keepdims=True)
                 top = top.astype(jnp.bfloat16).astype(jnp.float32)
@@ -214,14 +219,20 @@
                     e.astype(jnp.bfloat16), vbuf[:, pl.ds(col, HD)],
                     preferred_element_type=jnp.float32,
                 )
-                at = pl.multiple_of(j * wide + h * HD, HD)
+                at = j * wide + h * HD
+                at = at if isinstance(at, int) else pl.multiple_of(at, HD)
                 acc[pl.ds(first, tile_slots), :, pl.ds(at, HD)] = out.reshape(tile_slots, tok, HD)
                 stats = jnp.where(lane == h, top, stats)
                 return jnp.where(lane == h + HALF, mass, stats)
 
-            stats = lax.fori_loop(
-                0, hc, head, jnp.zeros((r, LANES), jnp.float32), unroll=tiles == 1
-            )
+            stats = jnp.zeros((r, LANES), jnp.float32)
+            if tiles == 1:
+                ahead = scores(0)
+                for h in range(hc):
+                    now, ahead = ahead, scores(h + 1) if h + 1 < hc else None
+                    stats = head(h, stats, now)
+            else:
+                stats = lax.fori_loop(0, hc, lambda h, st: head(h, st, scores(h)), stats)
             acc[pl.ds(first, tile_slots), :, pl.ds(j * wide + width, LANES)] = stats.reshape(
                 tile_slots, tok, LANES
             )

time: 32.6 us -> 30.5 us (0.936)
  Pallas kernels: 31.1 us -> 28.9 us
    pallas_call x1, Pallas kernels: 31.1 us -> 28.9 us  [per_device(): pl.pallas_call(functools.partial(kernel, dims, chunks), out_shape=jax.Sha...]
where the time goes in v3:
time: 30.5 us; the launch traced here: 30.4 us
  Pallas kernels  28.9 us (95%)
  local copies, waits for them, and re-layouts  1.4 us (5%)
    pallas_call x1, Pallas kernels, per_device(): pl.pallas_call(functools.partial(kernel, dims, chunks), out_shape=jax.Sha...  28.9 us
    unnamed x1, local copies, waits for them, and re-layouts  1.4 us

profile of v3, /device:TPU:0, one launch (start us, length us, event | category | flops | bytes accessed | tf_op | source)
XLA Modules:
  0.0 30.4 jit_solution(16119428136172952520)
XLA Ops:
  0.0 28.9 %shard_map.64 = bf16[8,2560]{1,0:T(8,128)(2,1)} custom-call(bf16[8,2560]{1,0:T(8,128)(2,1)} %q_hbm.1, bf16[8,2560]{1,0:T(8,128)(2,1)} %nk_hbm.1, bf16[8,2560]{1,0:T(8,128)(2,1)} %nv_hbm.1, s32[1,16]{1,0:T(1,128)} %bitcast.1, bf16[512,2560]{1,0:T(8,128)(2,1)} %ck_ref.1, bf16[512,2560]{1,0:T(8,128)(2,1)} %cv_ref.1), custom_call_target="tpu_custom_call" | custom-call | tf_op jit(solution)/shard_map/pallas_call | solution.py:398
  29.0 1.4 %copy.8 = bf16[8,2560]{1,0:T(8,128)(2,1)} copy(bf16[8,2560]{1,0:T(8,128)(2,1)} %shard_map.64) | data formatting | bytes 81920
